TPU v7x, 32 devices: a whole 2x2x4 slice. The times are simulated.
32 devices in a mesh: seq: 4 (over y, x), dp: 2 (over core), mp: 4 (over z).
Axes of the slice: x: 2, y: 2, z: 4, core: 2. Of those that a mesh axis runs over, the one named last changes fastest.
Arguments:
- tokens: bfloat16 [8, 2048, 2048], P('dp', 'seq', 'mp'), may hold values from -6 to 6
- cotangent: bfloat16 [8, 2048, 2048], P('dp', 'seq', 'mp'), may hold values from -6 to 6
- domain_id: int32 [8], P('dp'), may hold values from 0 to 7
- domain_weight: int32 [8], replicated, may hold values from 1 to 4
- lower_level: int32 [2048], P('mp'), may hold values from 2 to 23
- norm_in: float32 [2048], P('mp'), may hold values from 0.1 to 1.9
- w_input: bfloat16 [2048, 2048], P(None, 'mp'), may hold values from -0.125 to 0.125
- w_forget: bfloat16 [2048, 2048], P(None, 'mp'), may hold values from -0.125 to 0.125
- w_gate_out: bfloat16 [2048, 2048], P(None, 'mp'), may hold values from -0.125 to 0.125
- out_gain: float32 [2048], P('mp'), may hold values from 0.1 to 1.9
- w_out: bfloat16 [2048, 2048], P('mp'), may hold values from -0.125 to 0.125
- norm_mid: float32 [2048], P('mp'), may hold values from 0.1 to 1.9
- w_gate: bfloat16 [2048, 5632], P(None, 'mp'), may hold values from -0.125 to 0.125
- w_up: bfloat16 [2048, 5632], P(None, 'mp'), may hold values from -0.125 to 0.125
- w_down: bfloat16 [5632, 2048], P('mp'), may hold values from -0.078125 to 0.078125
Outputs:
- mixed: bfloat16 [8, 2048, 2048], P('dp', 'seq', 'mp')
- grad_tokens: float32 [8, 2048, 2048], P('dp', 'seq', 'mp')
- grad_norm_in: float32 [2048], P('mp')
- grad_w_input: float32 [2048, 2048], P(None, 'mp')
- grad_w_forget: float32 [2048, 2048], P(None, 'mp')
- grad_w_gate_out: float32 [2048, 2048], P(None, 'mp')
- grad_out_gain: float32 [2048], P('mp')
- grad_w_out: float32 [2048, 2048], P('mp')
- grad_norm_mid: float32 [2048], P('mp')
- grad_w_gate: float32 [2048, 5632], P(None, 'mp')
- grad_w_up: float32 [2048, 5632], P(None, 'mp')
- grad_w_down: float32 [5632, 2048], P('mp')
All inputs are finite; a program needn't handle non-finite values.
Results may differ from a plain program's by a relative error of at most 0.0075.
The roundings to bfloat16 on the way count: a program that leaves them out, or rounds other values in their place, can miss the bound.
Values may be sent and summed in bfloat16 or wider, within the bound.
No kernel may reach another device: no remote copies, remote signals or barrier semaphores. Data moves between devices by JAX's collectives and lax.ppermute only.
A program may use at most 320 MiB of HBM per device.

v0:
```python
import jax
import jax.numpy as jnp
from jax import lax
from jax.sharding import PartitionSpec as P

EPS = 1e-06


def entering(value, axis, join, neutral, backward):
    count, mine = (lax.axis_size(axis), lax.axis_index(axis))
    pieces = jax.tree.map(lambda part: lax.all_gather(part, axis), value)
    if backward:
        pieces = jax.tree.map(lambda part: part[::-1], pieces)
        mine = count - 1 - mine
    so_far = jax.tree.map(
        lambda part, zero: jnp.full_like(part, 0) + jnp.asarray(zero, part.dtype), value, neutral
    )

    def lap(position, so_far):
        longer = join(so_far, jax.tree.map(lambda part: part[position], pieces))
        return jax.tree.map(lambda new, old: jnp.where(position < mine, new, old), longer, so_far)

    return lax.fori_loop(0, count - 1, lap, so_far)


def row_total(values):
    return lax.psum(values, "mp")


def chain_pairs(earlier, later):
    return (earlier[0] * later[0], later[0] * earlier[1] + later[1])


def swish_slope(values):
    sigma = jax.nn.sigmoid(values)
    return sigma * (1.0 + values * (1.0 - sigma))


def contract_rows(left, right):
    return lax.dot_general(
        left, right, (((0,), (0,)), ((), ())), preferred_element_type=jnp.float32
    )


def contract_last(left, right):
    return lax.dot_general(
        left, right, (((1,), (1,)), ((), ())), preferred_element_type=jnp.float32
    )


def per_device(
    tokens,
    cotangent,
    domain_id,
    domain_weight,
    lower_level,
    norm_in,
    w_input,
    w_forget,
    w_gate_out,
    out_gain,
    w_out,
    norm_mid,
    w_gate,
    w_up,
    w_down,
):
    seq_count, block_len, own_width = tokens.shape
    row_count = seq_count * block_len
    full_width = own_width * lax.axis_size("mp")
    ff_local = w_gate.shape[1]
    x_rows = tokens.astype(jnp.float32).reshape(row_count, own_width)
    scale_in = lax.rsqrt(row_total(jnp.sum(x_rows * x_rows, 1)) / full_width + EPS)[:, None]
    x_hat = x_rows * scale_in
    normed_full = lax.all_gather((x_hat * norm_in).astype(jnp.bfloat16), "mp", axis=1, tiled=True)
    w_mix = jnp.concatenate((w_input, w_forget, w_gate_out), 1)
    projected = jnp.dot(normed_full, w_mix, preferred_element_type=jnp.float32)
    in_raw = projected[:, :own_width]
    forget_raw = projected[:, own_width : 2 * own_width]
    gate_raw = projected[:, 2 * own_width :]
    lower = 1.0 - jnp.exp2(-0.5 * lower_level.astype(jnp.float32))
    forget_sig = jax.nn.sigmoid(forget_raw)
    forget = lower + (1.0 - lower) * forget_sig
    in_act = jax.nn.silu(in_raw)
    inflow = in_act * (1.0 - forget)
    forget_seq = forget.reshape(seq_count, block_len, own_width)
    decay_run, state_run = lax.associative_scan(
        chain_pairs, (forget_seq, inflow.reshape(seq_count, block_len, own_width)), axis=1
    )
    unit_decay = jnp.ones((seq_count, own_width), jnp.float32)
    zero_state = jnp.zeros((seq_count, own_width), jnp.float32)
    carried_in = entering(
        (decay_run[:, -1], state_run[:, -1]), "seq", chain_pairs, (unit_decay, zero_state), False
    )
    state_in = carried_in[1]
    state_seq = state_run + decay_run * state_in[:, None, :]
    state = state_seq.reshape(row_count, own_width)
    scale_state = lax.rsqrt(row_total(jnp.sum(state * state, 1)) / full_width + EPS)[:, None]
    state_hat = state * scale_state
    gate_act = jax.nn.silu(gate_raw)
    gated = (state_hat * out_gain * gate_act).astype(jnp.bfloat16)
    out_cols = lax.all_to_all(w_out, "mp", split_axis=1, concat_axis=0, tiled=True)
    gated_full = lax.all_gather(gated, "mp", axis=1, tiled=True)
    branch = jnp.dot(gated_full, out_cols, preferred_element_type=jnp.float32)
    resid = x_rows + branch
    scale_mid = lax.rsqrt(row_total(jnp.sum(resid * resid, 1)) / full_width + EPS)[:, None]
    resid_hat = resid * scale_mid
    second_full = lax.all_gather(
        (resid_hat * norm_mid).astype(jnp.bfloat16), "mp", axis=1, tiled=True
    )
    w_pair = jnp.concatenate((w_gate, w_up), 1)

    def glu_inner(source):
        both = jnp.dot(source, w_pair, preferred_element_type=jnp.float32)
        return (both[:, :ff_local], both[:, ff_local:])

    gate_value, up_value = glu_inner(second_full)
    hidden_act = (jax.nn.silu(gate_value) * up_value).astype(jnp.bfloat16)
    glu_term = lax.psum_scatter(
        jnp.dot(hidden_act, w_down, preferred_element_type=jnp.float32),
        "mp",
        scatter_dimension=1,
        tiled=True,
    )
    block_out = resid + glu_term
    mixed = block_out.astype(jnp.bfloat16).reshape(seq_count, block_len, own_width)
    domain_hits = domain_id[:, None] == jnp.arange(domain_weight.shape[0], dtype=jnp.int32)[None, :]
    seq_weight = jnp.sum(jnp.where(domain_hits, domain_weight[None, :], 0), 1).astype(jnp.float32)
    grad_out = (cotangent.astype(jnp.float32) * seq_weight[:, None, None]).reshape(
        row_count, own_width
    )
    grad_out_full = lax.all_gather(grad_out.astype(jnp.bfloat16), "mp", axis=1, tiled=True)
    grad_hidden = contract_last(grad_out_full, w_down)
    grad_w_down = contract_rows(hidden_act, grad_out_full)
    gate_back, up_back = glu_inner(lax.optimization_barrier(second_full))
    gate_sigma = jax.nn.sigmoid(gate_back)
    grad_gate = (
        grad_hidden * up_back * gate_sigma * (1.0 + gate_back * (1.0 - gate_sigma))
    ).astype(jnp.bfloat16)
    grad_up = (grad_hidden * gate_back * gate_sigma).astype(jnp.bfloat16)
    grad_pair = jnp.concatenate((grad_gate, grad_up), 1)
    grad_w_pair = contract_rows(second_full, grad_pair)
    grad_second = lax.psum_scatter(
        contract_last(grad_pair, w_pair), "mp", scatter_dimension=1, tiled=True
    )
    grad_norm_mid = jnp.sum(grad_second * resid_hat, 0)
    grad_mid_hat = grad_second * norm_mid
    mid_dot = row_total(jnp.sum(grad_mid_hat * resid_hat, 1))[:, None] / full_width
    grad_resid = grad_out + scale_mid * (grad_mid_hat - resid_hat * mid_dot)
    grad_resid_full = lax.all_gather(grad_resid.astype(jnp.bfloat16), "mp", axis=1, tiled=True)
    grad_w_out = contract_rows(gated, grad_resid_full)
    grad_gated = contract_last(grad_resid_full, w_out)
    grad_out_gain = jnp.sum(grad_gated * state_hat * gate_act, 0)
    grad_gate_raw = (grad_gated * state_hat * out_gain * swish_slope(gate_raw)).astype(jnp.bfloat16)
    grad_state_hat = grad_gated * out_gain * gate_act
    state_dot = row_total(jnp.sum(grad_state_hat * state_hat, 1))[:, None] / full_width
    grad_state = scale_state * (grad_state_hat - state_hat * state_dot)
    grad_state_seq = grad_state.reshape(seq_count, block_len, own_width)
    back_decay, back_run = lax.associative_scan(
        chain_pairs, (forget_seq, forget_seq * grad_state_seq), reverse=True, axis=1
    )
    carried_back = entering(
        (back_decay[:, 0], back_run[:, 0]), "seq", chain_pairs, (unit_decay, zero_state), True
    )
    later_in = carried_back[1]
    passed = back_run + back_decay * later_in[:, None, :]
    adjoint_seq = grad_state_seq + jnp.concatenate((passed[:, 1:], later_in[:, None, :]), 1)
    prev_state = jnp.concatenate((state_in[:, None, :], state_seq[:, :-1]), 1)
    adjoint = adjoint_seq.reshape(row_count, own_width)
    prev_rows = prev_state.reshape(row_count, own_width)
    grad_forget = adjoint * prev_rows - adjoint * in_act
    grad_in_raw = (adjoint * (1.0 - forget) * swish_slope(in_raw)).astype(jnp.bfloat16)
    grad_forget_raw = (grad_forget * (1.0 - lower) * forget_sig * (1.0 - forget_sig)).astype(
        jnp.bfloat16
    )
    grad_projected = jnp.concatenate((grad_in_raw, grad_forget_raw, grad_gate_raw), 1)
    grad_w_mix = contract_rows(normed_full, grad_projected)
    grad_normed = lax.psum_scatter(
        contract_last(grad_projected, w_mix), "mp", scatter_dimension=1, tiled=True
    )
    grad_norm_in = jnp.sum(grad_normed * x_hat, 0)
    grad_in_hat = grad_normed * norm_in
    in_dot = row_total(jnp.sum(grad_in_hat * x_hat, 1))[:, None] / full_width
    grad_tokens = grad_resid + scale_in * (grad_in_hat - x_hat * in_dot)
    totals = lax.psum(
        (
            grad_norm_in,
            grad_w_mix[:, :own_width],
            grad_w_mix[:, own_width : 2 * own_width],
            grad_w_mix[:, 2 * own_width :],
            grad_out_gain,
            grad_w_out,
            grad_norm_mid,
            grad_w_pair[:, :ff_local],
            grad_w_pair[:, ff_local:],
            grad_w_down,
        ),
        ("seq", "dp"),
    )
    return (
        mixed,
        grad_tokens.reshape(seq_count, block_len, own_width),
        totals[0],
        totals[1],
        totals[2],
        totals[3],
        totals[4],
        totals[5],
        totals[6],
        totals[7],
        totals[8],
        totals[9],
    )


def solution(mesh):
    in_specs = (
        P("dp", "seq", "mp"),
        P("dp", "seq", "mp"),
        P("dp"),
        P(),
        P("mp"),
        P("mp"),
        P(None, "mp"),
        P(None, "mp"),
        P(None, "mp"),
        P("mp"),
        P("mp", None),
        P("mp"),
        P(None, "mp"),
        P(None, "mp"),
        P("mp", None),
    )
    out_specs = (
        P("dp", "seq", "mp"),
        P("dp", "seq", "mp"),
        P("mp"),
        P(None, "mp"),
        P(None, "mp"),
        P(None, "mp"),
        P("mp"),
        P("mp", None),
        P("mp"),
        P(None, "mp"),
        P(None, "mp"),
        P("mp", None),
    )
    return jax.shard_map(
        per_device, mesh=mesh, in_specs=in_specs, out_specs=out_specs, check_vma=False
    )
```

profile of v0, /device:TPU:0, one launch (start us, length us, event | category | flops | bytes accessed | tf_op | source)
XLA Modules:
  0.0 3188.6 jit_solution(3619002101023223962)
XLA Ops:
  9.5 13.7 psum.112
  32.6 142.7 %all-gather.10.cloned.1.call-done = bf16[2048,2048]{1,0:T(8,128)(2,1)} async-done(((bf16[2048,512]{1,0:T(8,128)(2,1)}), bf16[2048,2048]{1,0:T(8,128)(2,1)}) %all-gather.10.cloned.1.call-update) | async-done | bytes 8388624 | tf_op jit(solution)/shard_map/all_gather | solution.py:75
  175.3 17.4 fusion.66
  233.5 12.0 slice.600
  372.6 12.0 slice.660
  384.6 12.0 slice.595
  525.9 103.9 %all_to_all.19 = bf16[512,4,512]{0,2,1:T(8,128)(2,1)} all-to-all(bf16[512,4,512]{0,2,1:T(8,128)(2,1)} %bitcast.155), channel_id=1, replica_groups=mesh['seq'=4,'dp'=2,'mp'=4] {'mp'}, dimensions={1} | all-to-all | bytes 4194304 | tf_op jit(solution)/shard_map/all_to_all | solution.py:102
  633.9 74.8 %all-gather.12.cloned.1.call-done = bf16[2048,2048]{1,0:T(8,128)(2,1)} async-done(((bf16[2048,512]{1,0:T(8,128)(2,1)}), bf16[2048,2048]{1,0:T(8,128)(2,1)}) %all-gather.12.cloned.1.call-update) | async-done | bytes 8388624 | tf_op jit(solution)/shard_map/all_gather | solution.py:103
  750.8 130.4 %all-gather.14.cloned.1.call-done = bf16[2048,2048]{1,0:T(8,128)(2,1)} async-done(((bf16[2048,512]{1,0:T(8,128)(2,1)}), bf16[2048,2048]{1,0:T(8,128)(2,1)}) %all-gather.14.cloned.1.call-update) | async-done | bytes 8388624 | tf_op jit(solution)/shard_map/all_gather | solution.py:108
  881.2 32.0 %fusion.69 = f32[2048,2816]{1,0:T(8,128)} fusion(bf16[2048,2048]{1,0:T(8,128)(2,1)} %all-gather.14.cloned.1.call-done, bf16[2048,2816]{1,0:T(8,128)(2,1)} %constant_dynamic-update-slice_fusion.3), kind=kOutput, calls=%fused_computation.224 | convolution fusion | flops 23622320128 | bytes 42991616 | tf_op jit(solution)/shard_map/dot_general | solution.py:114
  913.2 117.9 %all-gather.16.cloned.1.call-done = bf16[2048,2048]{1,0:T(8,128)(2,1)} async-done(((bf16[2048,512]{1,0:T(8,128)(2,1)}), bf16[2048,2048]{1,0:T(8,128)(2,1)}) %all-gather.16.cloned.1.call-update) | async-done | bytes 8388624 | tf_op jit(solution)/shard_map/all_gather | solution.py:132
  1031.1 24.2 fusion.4
  1055.2 31.9 %fusion.7 = f32[2048,2048]{1,0:T(8,128)} fusion(bf16[2048,2816]{1,0:T(8,128)(2,1)} %constant_dynamic-update-slice_fusion.3, bf16[2048,1408]{1,0:T(8,128)(2,1)} %get-tuple-element.281, bf16[2048,1408]{1,0:T(8,128)(2,1)} %get-tuple-element.280), kind=kOutput, calls=%fused_computation.16 | convolution fusion | flops 23645388800 | bytes 39845888 | tf_op jit(solution)/shard_map/dot_general | solution.py:46
  1087.3 30.6 fusion.67
  1124.0 19.4 fusion.68
  1143.4 222.4 %reduce-scatter.6.cloned.1.call-done = f32[2048,512]{1,0:T(8,128)} async-done(((f32[2048,2048]{1,0:T(8,128)}), f32[2048,512]{1,0:T(8,128)}) %reduce-scatter.6.cloned.1.call-update) | async-done | bytes 4194320 | tf_op jit(solution)/shard_map/reduce_scatter | solution.py:143
  1382.1 267.3 %reduce-scatter.4.cloned.1.call-done = f32[2048,512]{1,0:T(8,128)} async-done(((f32[2048,2048]{1,0:T(8,128)}), f32[2048,512]{1,0:T(8,128)}) %reduce-scatter.4.cloned.1.call-update) | async-done | bytes 4194320 | tf_op jit(solution)/shard_map/reduce_scatter | solution.py:119
  1659.5 16.9 slice.688
  1713.4 96.8 %all-gather.18.cloned.1.call-done = bf16[2048,2048]{1,0:T(8,128)(2,1)} async-done(((bf16[2048,512]{1,0:T(8,128)(2,1)}), bf16[2048,2048]{1,0:T(8,128)(2,1)}) %all-gather.18.cloned.1.call-update) | async-done | bytes 8388624 | tf_op jit(solution)/shard_map/all_gather | solution.py:150
  1810.2 13.0 multiply_reduce_fusion.1
  1866.3 16.6 slice.692
  2056.4 17.1 slice.755
  2155.7 32.5 %rev.14 = f32[4,512,512]{2,1,0:T(8,128)} reverse(f32[4,512,512]{2,1,0:T(8,128)} %add.592), dimensions={1} | reverse | bytes 8388608 | tf_op jit(solution)/shard_map/rev | solution.py:159
  2188.2 32.5 %rev.15 = f32[4,512,512]{2,1,0:T(8,128)} reverse(f32[4,512,512]{2,1,0:T(8,128)} %add.601), dimensions={1} | reverse | bytes 8388608 | tf_op jit(solution)/shard_map/rev | solution.py:159
  2237.0 18.9 fusion.31
  2256.0 33.5 %fusion.6 = f32[2048,2816]{1,0:T(8,128)} fusion(bf16[2048,2048]{1,0:T(8,128)(2,1)} %all-gather.14.cloned.1.call-done, bf16[2048,1408]{1,0:T(8,128)(2,1)} %get-tuple-element.281, bf16[2048,1408]{1,0:T(8,128)(2,1)} %get-tuple-element.280), kind=kOutput, calls=%fused_computation.15 | convolution fusion | flops 23645388800 | bytes 42991616 | tf_op jit(solution)/shard_map/dot_general | solution.py:40
  2289.5 17.2 fusion.59
  2306.6 19.2 fusion.71
  2325.8 17.0 fusion.30
  2362.5 172.1 %reduce-scatter.8.cloned.1.call-done = f32[2048,512]{1,0:T(8,128)} async-done(((f32[2048,2048]{1,0:T(8,128)}), f32[2048,512]{1,0:T(8,128)}) %reduce-scatter.8.cloned.1.call-update) | async-done | bytes 4194320 | tf_op jit(solution)/shard_map/reduce_scatter | solution.py:178
  2537.5 14.4 all-reduce.72
  2569.2 568.9 %all-reduce.76.cloned.1.call-done = (f32[2048,512]{1,0:T(8,128)}, f32[2048,512]{1,0:T(8,128)}, f32[2048,512]{1,0:T(8,128)}, f32[512,2048]{1,0:T(8,128)}, f32[204...) async-done(((f32[2048,512]{1,0:T(8,128)}, f32[2048,512]{1,0:T(8,128)}, f32[2048,512]{1,0:T(8,128)}, f32[512,2048]{1,0:T(8,128)}, f32[2048,1408]{1,0:T(8,128)}, ...) | async-done | bytes 51380240 | tf_op jit(solution)/shard_map/psum | solution.py:185
  (610 shorter events, 821.6 us)
Async XLA Ops:
  7.2 168.1 %all-gather.10.cloned.1.call-start = ((), (), s32[]{:S(2)}) async-start(), calls=%async_computation.4 | async-start | bytes 10485760 | tf_op jit(solution)/shard_map/all_gather | solution.py:75
  27.3 681.5 %all-gather.12.cloned.1.call-start = ((), (), s32[]{:S(2)}) async-start(), calls=%async_computation.5 | async-start | bytes 10485760 | tf_op jit(solution)/shard_map/all_gather | solution.py:103
  27.4 165.3 %copy-start.104 = (f32[512]{0:T(512)}, f32[512]{0:T(512)S(1)}, u32[]{:S(2)}) copy-start(f32[512]{0:T(512)S(1)} %get-tuple-element.371) | copy-start | bytes 6148
  251.4 29.6 copy-start.17
  372.5 27.1 copy-start.100
  372.5 27.2 copy-start.70
  372.5 27.3 copy-start.69
  372.5 27.5 copy-start.61
  372.5 27.5 copy-start.62
  372.5 27.5 copy-start.90
  372.5 27.6 copy-start.89
  372.5 27.7 copy-start.53
  372.6 27.7 copy-start.54
  523.3 357.9 %all-gather.14.cloned.1.call-start = ((), (), s32[]{:S(2)}) async-start(), calls=%async_computation.6 | async-start | bytes 10485760 | tf_op jit(solution)/shard_map/all_gather | solution.py:108
  525.9 182.8 %copy-start.6 = (bf16[4,512,512]{2,1,0:T(8,128)(2,1)S(1)}, bf16[4,512,512]{2,1,0:T(8,128)(2,1)}, u32[]{:S(2)}) copy-start(bf16[4,512,512]{2,1,0:T(8,128)(2,1)} %param.19) | copy-start | bytes 6291460
  734.2 296.9 %all-gather.16.cloned.1.call-start = ((), (), s32[]{:S(2)}) async-start(), calls=%async_computation.8 | async-start | bytes 10485760 | tf_op jit(solution)/shard_map/all_gather | solution.py:132
  738.8 627.1 %reduce-scatter.6.cloned.1.call-start = ((), (), s32[]{:S(2)}) async-start(), calls=%async_computation.9 | async-start | bytes 20971520 | tf_op jit(solution)/shard_map/reduce_scatter | solution.py:143
  1087.2 562.2 %reduce-scatter.4.cloned.1.call-start = ((), (), s32[]{:S(2)}) async-start(), calls=%async_computation.7 | async-start | bytes 20971520 | tf_op jit(solution)/shard_map/reduce_scatter | solution.py:119
  1143.3 222.5 %copy-start.64 = (f32[2048]{0:T(1024)S(1)}, f32[2048]{0:T(1024)}, u32[]{:S(2)}) copy-start(f32[2048]{0:T(1024)} %copy-done.63) | copy-start | bytes 24580
  1143.3 222.5 %copy-start.103 = (f32[512]{0:T(512)S(1)}, f32[512]{0:T(512)}, u32[]{:S(2)}) copy-start(f32[512]{0:T(512)} %param.30) | copy-start | bytes 6148
  1143.4 666.8 %all-gather.18.cloned.1.call-start = ((), (), s32[]{:S(2)}) async-start(), calls=%async_computation.10 | async-start | bytes 10485760 | tf_op jit(solution)/shard_map/all_gather | solution.py:150
  1659.5 875.0 %reduce-scatter.8.cloned.1.call-start = ((), (), s32[]{:S(2)}) async-start(), calls=%async_computation.11 | async-start | bytes 20971520 | tf_op jit(solution)/shard_map/reduce_scatter | solution.py:178
  1708.3 101.9 %copy-start.39 = (bf16[512,2048]{1,0:T(8,128)(2,1)S(1)}, bf16[512,2048]{1,0:T(8,128)(2,1)}, u32[]{:S(2)}) copy-start(bf16[512,2048]{1,0:T(8,128)(2,1)} %param.29) | copy-start | bytes 6291460
  1708.3 101.9 %copy-start.66 = (f32[2048]{0:T(1024)S(1)}, f32[2048]{0:T(1024)}, u32[]{:S(2)}) copy-start(f32[2048]{0:T(1024)} %copy-done.65) | copy-start | bytes 24580
  1708.3 101.9 %copy-start.107 = (f32[512]{0:T(512)S(1)}, f32[512]{0:T(512)}, u32[]{:S(2)}) copy-start(f32[512]{0:T(512)} %param.28) | copy-start | bytes 6148
  2255.9 882.2 %all-reduce.76.cloned.1.call-start = ((), (), s32[]{:S(2)}) async-start(), calls=%async_computation.12 | async-start | bytes 102760448 | tf_op jit(solution)/shard_map/psum | solution.py:185
  2289.5 36.4 %slice-start = ((s8[8388608]{0:T(1024)(128)(4,1)}), s8[4194304]{0:T(1024)(128)(4,1)S(1)}, s32[]{:S(2)}) async-start(s8[8388608]{0:T(1024)(128)(4,1)} %bitcast.195), calls=%async_computation.13 | async-start | bytes 8388608
  2362.4 172.1 %copy-start.7 = (bf16[4,512,512]{2,1,0:T(8,128)(2,1)S(1)}, bf16[4,512,512]{2,1,0:T(8,128)(2,1)}, u32[]{:S(2)}) copy-start(bf16[4,512,512]{2,1,0:T(8,128)(2,1)} %param.19) | copy-start | bytes 6291460
  2362.4 172.1 %copy-start.58 = (f32[2048]{0:T(1024)S(1)}, f32[2048]{0:T(1024)}, u32[]{:S(2)}) copy-start(f32[2048]{0:T(1024)} %copy-done.57) | copy-start | bytes 24580
  2362.4 172.1 %copy-start.101 = (f32[512]{0:T(512)S(1)}, f32[512]{0:T(512)}, u32[]{:S(2)}) copy-start(f32[512]{0:T(512)} %param.24) | copy-start | bytes 6148
  2362.4 175.0 %copy-start.108 = (f32[512]{0:T(512)S(1)}, f32[512]{0:T(512)}, u32[]{:S(2)}) copy-start(f32[512]{0:T(512)} %get-tuple-element.240) | copy-start | bytes 6148
  2362.4 175.0 %copy-start.110 = (f32[512]{0:T(512)S(1)}, f32[512]{0:T(512)}, u32[]{:S(2)}) copy-start(f32[512]{0:T(512)} %get-tuple-element.238) | copy-start | bytes 6148
  (92 other events, 935.7 us)
Sparse Core Ops, SparseCore 0:
  27.4 147.8 all-gather.9
  523.5 185.2 all-gather.11
  734.3 146.8 all-gather.13
  883.2 147.8 all-gather.15
  1087.3 278.4 reduce-scatter.5
  1368.2 281.2 reduce-scatter.3
  1659.6 150.5 all-gather.17
  2256.0 278.4 reduce-scatter.7
  2541.6 596.4 all-reduce.75
where the time goes:
time: 3220 us; the launch traced here: 3190 us
  waiting for transfers between devices  1790 us (56%)
  local copies, waits for them, and re-layouts  679 us (21%)
  matrix products  277 us (9%)
  blocking collectives  216 us (7%)
  other arithmetic  206 us (6%)
    psum x1, waiting for transfers between devices, per_device(): lax.psum((grad_norm_in, grad_w_mix[:, :own_width], grad_w_mix[:, own_widt...  569 us
    reduce_scatter x1, waiting for transfers between devices, per_device(): lax.psum_scatter(jnp.dot(hidden_act, w_down, preferred_element_type=jnp.f...  267 us
    slice x64, local copies, waits for them, and re-layouts, per_device(): lax.associative_scan(chain_pairs, (forget_seq, forget_seq * grad_state_se...  229 us
    reduce_scatter x1, waiting for transfers between devices, per_device(): lax.psum_scatter(contract_last(grad_pair, w_pair), 'mp', scatter_dimensio...  222 us
    slice x59, local copies, waits for them, and re-layouts, per_device(): lax.associative_scan(chain_pairs, (forget_seq, inflow.reshape(seq_count,...  176 us
    reduce_scatter x1, waiting for transfers between devices, per_device(): lax.psum_scatter(contract_last(grad_projected, w_mix), 'mp', scatter_dime...  172 us
    all_gather x1, waiting for transfers between devices, per_device(): lax.all_gather((x_hat * norm_in).astype(jnp.bfloat16), 'mp', axis=1, tile...  143 us
    all_gather x1, waiting for transfers between devices, per_device(): lax.all_gather((resid_hat * norm_mid).astype(jnp.bfloat16), 'mp', axis=1,...  130 us
  transfers between devices with their start and end apart: 9, of which 9 were waited for; matrix products, arithmetic and copies ran while one was open for 9% of the time, Pallas kernels for 0%

commit v1 on v0

v1 whole, which is shorter than its diff:
```python
import jax
import jax.numpy as jnp
from jax import lax
from jax.experimental import pallas as pl
from jax.experimental.pallas import tpu as pltpu
from jax.sharding import PartitionSpec as P

EPS = 1e-06
F32 = jnp.float32
BF16 = jnp.bfloat16
LANES = 8


def scan_body(backward, a_ref, b_ref, d_ref, e_ref, td_ref, te_ref):
    seqs, count, width = a_ref.shape
    seg = count // LANES

    def step(j, carry):
        at = seg - 1 - j if backward else j
        rows = pl.ds(at, LANES, stride=seg)
        after = []
        for i, (decay, run) in enumerate(carry):
            d_ref[i, rows, :] = decay
            e_ref[i, rows, :] = run
            factor = a_ref[i, rows, :]
            after.append((factor * decay, factor * run + b_ref[i, rows, :]))
        return tuple(after)

    start = (jnp.ones((LANES, width), F32), jnp.zeros((LANES, width), F32))
    ends = lax.fori_loop(0, seg, step, (start,) * seqs, unroll=4)
    for i, (decay, run) in enumerate(ends):
        carry_d = jnp.ones((1, width), F32)
        carry_e = jnp.zeros((1, width), F32)
        for g in reversed(range(LANES)) if backward else range(LANES):
            rows = pl.ds(g * seg, seg)
            inner = d_ref[i, rows, :]
            e_ref[i, rows, :] = e_ref[i, rows, :] + inner * carry_e
            d_ref[i, rows, :] = inner * carry_d
            own_d, own_e = (decay[g : g + 1, :], run[g : g + 1, :])
            carry_d, carry_e = (carry_d * own_d, own_d * carry_e + own_e)
        td_ref[i] = carry_d
        te_ref[i] = carry_e


def linear_scan(factor, term, backward):
    seqs, count, width = factor.shape
    lanes = 128
    block = pl.BlockSpec((seqs, count, lanes), lambda i: (0, 0, i))
    last = pl.BlockSpec((seqs, 1, lanes), lambda i: (0, 0, i))
    whole = jax.ShapeDtypeStruct(factor.shape, F32)
    total = jax.ShapeDtypeStruct((seqs, 1, width), F32)
    return pl.pallas_call(
        lambda *refs: scan_body(backward, *refs),
        grid=(width // lanes,),
        in_specs=[block, block],
        out_specs=[block, block, last, last],
        out_shape=[whole, whole, total, total],
        name="scan_back" if backward else "scan_fwd",
    )(factor, term)


def dot(left, right):
    return jnp.dot(left, right, preferred_element_type=F32)


def dot_t(left, right):
    return lax.dot_general(left, right, (((1,), (1,)), ((), ())), preferred_element_type=F32)


def t_dot(left, right):
    return lax.dot_general(left, right, (((0,), (0,)), ((), ())), preferred_element_type=F32)


def sigmoid(v):
    return jax.nn.sigmoid(v)


def after(value, *earlier):
    return lax.optimization_barrier((value, earlier))[0]


def bits_of(count):
    return [1 << i for i in range(count.bit_length() - 1)]


def per_device(
    tokens,
    cotangent,
    domain_id,
    domain_weight,
    lower_level,
    norm_in,
    w_input,
    w_forget,
    w_gate_out,
    out_gain,
    w_out,
    norm_mid,
    w_gate,
    w_up,
    w_down,
):
    n_seq, n_core, n_mp = (lax.axis_size(axis) for axis in ("seq", "dp", "mp"))
    assert n_core == 2
    half = n_mp // 2
    group = n_mp
    seqs, length, width = tokens.shape
    rows = seqs * length
    chunk = rows // group
    full = width * n_mp
    block = full // n_seq
    ff = w_gate.shape[1]
    s, c, m = (lax.axis_index(axis) for axis in ("seq", "dp", "mp"))
    part, low = (m // half, m % half)
    q = low + half * (part ^ c)
    v = low + half * c

    group_bits = bits_of(half) + [half]

    def hop(value, bit):
        if bit == half:
            return lax.ppermute(value, "dp", [(0, 1), (1, 0)])
        return lax.ppermute(value, "mp", [(i, i ^ bit) for i in range(n_mp)])

    def gather_group(value):
        pieces = {0: value}
        for bit in group_bits:
            for k in list(pieces):
                pieces[k | bit] = hop(pieces[k], bit)
        return [pieces[k] for k in range(group)]

    remote_first = sorted(range(group), key=lambda k: (-(k % half), k // half == 0))

    def scatter_group(partial, holds, fill):
        live = dict(partial)
        for bit in reversed(group_bits):
            for k in [k for k in remote_first if k in live and k & bit]:
                sent = live.pop(k).astype(BF16)
                if len(live) == 1:
                    holds = fill(sent) if callable(fill) else fill
                received = after(hop(sent, bit), holds)
                live[k ^ bit] = live[k ^ bit] + received.astype(F32)
        return live[0], sent

    def sum_group(value, fill=()):
        for bit in group_bits:
            value = value + after(hop(value, bit), fill if bit == half else ())
        return value

    def place(core, at):
        return core * n_mp + at

    crossing = [
        (place(core, at), place(1 - core, at ^ half))
        for core in range(2)
        for at in range(n_mp)
        if at // half != core
    ]

    def to_native(value, fill=()):
        got = after(lax.ppermute(value, ("dp", "mp"), crossing), fill)
        return jnp.where(c == part, value, got)

    seq_bits = len(bits_of(n_seq))
    straight = list(range(seq_bits))
    crossed = straight[::-1]

    def rows_of(value, at, count):
        return lax.dynamic_slice_in_dim(value, at * count, count, 0)

    def cols_of(value, at, count):
        return lax.dynamic_slice_in_dim(value, at * count, count, 1)

    def join(parts, spot, count, shape, axis, dtype):
        total = jnp.zeros(shape, dtype)
        for k, value in enumerate(parts):
            total = lax.dynamic_update_slice_in_dim(total, value, spot(k) * count, axis)
        return total

    def fetch_start(*own):
        count = own[0].shape[0] // (2 * n_seq)
        pieces = [rows_of(value, s * 2 + c, count) for value in own]
        return lax.ppermute(jnp.concatenate(pieces, 1), "mp", [(i, i ^ half) for i in range(n_mp)])

    def fetch_end(piece, *own):
        there = lax.all_gather(piece, ("seq", "dp"), axis=0, tiled=True)
        whole, at = ([], 0)
        for value in own:
            wide = value.shape[1]
            whole.append(jnp.where(c == 1, there[:, at : at + wide], value))
            at += wide
        return whole

    def total_of(left, right):
        return (left.astype(F32) + right.astype(F32)).astype(BF16)

    def sync(value, order, gates):
        height, wide = value.shape
        value = value.reshape((2,) * seq_bits + (height // n_seq, wide))
        left = crossed.copy()
        for bit, gate in zip(order, gates, strict=True):
            axis = left.index(bit)
            here = (s >> bit) & 1
            away = lax.dynamic_index_in_dim(value, 1 - here, axis, keepdims=False)
            kept = lax.dynamic_index_in_dim(value, here, axis, keepdims=False)
            away = lax.ppermute(away, "seq", [(i, i ^ (1 << bit)) for i in range(n_seq)])
            value = total_of(kept, after(away, gate))
            left.remove(bit)
        return value

    def combine(value, gate, gate_core):
        other = lax.ppermute(
            value, ("dp", "mp"), [(place(1, i), place(0, i ^ half)) for i in range(n_mp)]
        )
        value = total_of(value, after(other, gate))
        cut = value.shape[0] // 2
        lower_part = after(lax.ppermute(value[cut:], "dp", [(0, 1)]), gate_core)
        return jnp.where(c == 0, value[:cut], lower_part)

    def spread(value):
        return lax.all_gather(value, ("seq", "dp"), axis=0, tiled=True)

    small = jnp.stack((norm_in, norm_mid, out_gain, lower_level.astype(F32)))
    small = small[None]
    for bit in bits_of(n_mp):
        there = lax.ppermute(small, "mp", [(i, i ^ bit) for i in range(n_mp)])
        small = jnp.concatenate((small, there), 0)

    def small_of(at, row):
        return lax.dynamic_index_in_dim(small[:, row], m ^ at, 0, keepdims=False)

    gain_mid = jnp.concatenate([small_of(k, 1) for k in range(n_mp)])
    gain_out = small_of(q, 2)
    lower_level = small_of(q, 3)
    lower = 1.0 - jnp.exp2(-0.5 * lower_level)
    domain_hits = domain_id[:, None] == jnp.arange(domain_weight.shape[0], dtype=jnp.int32)[None, :]
    seq_weight = jnp.sum(jnp.where(domain_hits, domain_weight[None, :], 0), 1).astype(F32)
    seq_weight = jnp.where(c == part, seq_weight, lax.ppermute(seq_weight, "dp", [(0, 1), (1, 0)]))
    row_weight = jnp.broadcast_to(seq_weight[:, None], (seqs, length)).reshape(rows, 1)

    mix_piece = fetch_start(w_input, w_forget, w_gate_out)
    x_own = to_native(tokens.reshape(rows, width))
    mix_piece, x_own = lax.optimization_barrier((mix_piece, x_own))
    x_parts = gather_group(x_own)
    w_in, w_fg, w_go = fetch_end(mix_piece, w_input, w_forget, w_gate_out)
    out_piece = fetch_start(after(w_out, x_own))
    pair_piece = fetch_start(*after((w_gate, w_up), x_own))
    out_piece, pair_piece, x_parts[1] = lax.optimization_barrier((out_piece, pair_piece, x_parts[1]))
    x_parts[1] = after(x_parts[1], w_in, w_fg, w_go)
    (out_w,) = fetch_end(out_piece, w_out)
    gate_w, up_w = fetch_end(pair_piece, w_gate, w_up)
    squares = sum(jnp.sum(jnp.square(part_x.astype(F32)), 1) for part_x in x_parts)
    scale_in = lax.rsqrt(squares / full + EPS)[:, None]
    normed = join(
        [
            (
                part_x.astype(F32)
                * scale_in
                * small_of(v ^ k, 0)
            ).astype(BF16)
            for k, part_x in enumerate(x_parts)
        ],
        lambda k: v ^ k,
        width,
        (rows, full),
        1,
        BF16,
    )
    x_chunk = join(
        [rows_of(part_x, q, chunk) for part_x in x_parts],
        lambda k: v ^ k,
        width,
        (chunk, full),
        1,
        BF16,
    ).astype(F32)

    in_raw = dot(normed, w_in)
    forget_raw = dot(normed, w_fg)
    forget_sig = sigmoid(forget_raw)
    forget = lower + (1.0 - lower) * forget_sig
    in_sig = sigmoid(in_raw)
    in_act = in_raw * in_sig
    inflow = in_act * (1.0 - forget)
    gate_raw = dot(normed, w_go)
    shape3 = (seqs, length, width)

    def carry(decay, run, backward, fill=()):
        both = jnp.concatenate((decay, run), 1)
        total = jnp.zeros((seqs, width), F32)
        for d in range(n_seq - 1, 0, -1):
            step = -d if backward else d
            pairs = [(i, i + step) for i in range(n_seq) if 0 <= i + step < n_seq]
            got = after(lax.ppermute(both, "seq", pairs), fill)
            total = got[:, 0] * total + got[:, 1]
        return total[:, None, :]

    decay_run, state_run, decay_all, state_all = linear_scan(
        forget.reshape(shape3), inflow.reshape(shape3), False
    )
    state_in = carry(decay_all, state_all, False, (gate_raw,))
    prev = (state_run + decay_run * state_in).reshape(rows, width)
    state = forget * prev + inflow
    scale_state = lax.rsqrt(sum_group(jnp.sum(state * state, 1)) / full + EPS)[:, None]
    state_hat = state * scale_state
    gate_sig = sigmoid(gate_raw)
    gate_act = gate_raw * gate_sig
    gated = (state_hat * gain_out * gate_act).astype(BF16)
    branch_terms = {k: dot(rows_of(gated, q ^ k, chunk), out_w) for k in remote_first}
    branch, branch_sent = scatter_group(branch_terms, (), (branch_terms[0], gate_w, up_w))
    down_piece = fetch_start(after(w_down, branch_sent))
    cot_own = to_native(after(cotangent, branch_sent).reshape(rows, width), (branch,))
    down_piece, branch = lax.optimization_barrier((down_piece, branch))
    (down_w,) = fetch_end(down_piece, w_down)
    resid = x_chunk + branch
    scale_mid = lax.rsqrt(jnp.mean(resid * resid, 1, keepdims=True) + EPS)
    resid_hat = resid * scale_mid
    seconds = gather_group((resid_hat * gain_mid).astype(BF16))
    cot_parts = gather_group(after(cot_own, seconds[half]))

    hids, dzs, d_gates, d_ups, gates, acts = ([None] * group for _ in range(6))
    local_first = sorted(range(group), key=lambda k: (k % half, k))
    for k in local_first:
        local = (hids[0], hids[half]) if k % half else ()
        second = after(seconds[k], local)
        gates[k] = (dot(second, gate_w), dot(second, up_w))
        acts[k] = gates[k][0] * sigmoid(gates[k][0])
        hids[k] = (acts[k] * gates[k][1]).astype(BF16)
    cot_parts = [after(value, hids[0], hids[half]) if k % half else value for k, value in enumerate(cot_parts)]
    cot = join(cot_parts, lambda k: v ^ k, width, (rows, full), 1, BF16)
    d_seconds = {}
    for k in remote_first:
        remote = () if k % half else tuple(d_seconds[j] for j in remote_first if j % half)
        dzs[k] = (
            rows_of(cot, q ^ k, chunk).astype(F32) * rows_of(row_weight, q ^ k, chunk)
        ).astype(BF16)
        d_hid = dot_t(after(dzs[k], remote), down_w)
        gate, up = gates[k]
        sig = sigmoid(gate)
        d_gates[k] = (d_hid * up * (sig * (1.0 + gate * (1.0 - sig)))).astype(BF16)
        d_ups[k] = (d_hid * acts[k]).astype(BF16)
        d_seconds[k] = dot_t(d_gates[k], gate_w) + dot_t(d_ups[k], up_w)
    kept = []

    def fill(sent):
        kept.append(t_dot(jnp.concatenate(after(hids, sent), 0), jnp.concatenate(dzs, 0)).astype(BF16))
        return (kept[0], d_seconds[0])

    d_second, _ = scatter_group(d_seconds, (), fill)
    down_term = kept[0]

    grad_norm_mid = jnp.sum(d_second * resid_hat, 0)
    d_hat = d_second * gain_mid
    mid_dot = jnp.mean(d_hat * resid_hat, 1, keepdims=True)
    d_out = rows_of(cot, q, chunk).astype(F32) * rows_of(row_weight, q, chunk)
    d_resid = d_out + scale_mid * (d_hat - resid_hat * mid_dot)
    d_resids = gather_group(d_resid.astype(BF16))

    second_all = after(jnp.concatenate(seconds, 0), d_resids[0])
    d_pair = jnp.concatenate([jnp.concatenate((d_gates[k], d_ups[k]), 1) for k in range(group)], 0)
    pair_term = t_dot(second_all, d_pair).astype(BF16)
    d_resids = [
        after(value, pair_term) if k % half else value
        for k, value in enumerate(d_resids)
    ]

    def scatter_seq(value):
        return lax.psum_scatter(value, "seq", scatter_dimension=0, tiled=True)

    down_sum, pair_sum = (scatter_seq(value) for value in (down_term, pair_term))

    d_gated = join(
        [dot_t(value, out_w) for value in d_resids],
        lambda k: q ^ k,
        chunk,
        (rows, width),
        0,
        F32,
    )
    outs = {k: dot(after(hids[k], d_gated), down_w) for k in remote_first}
    grad_out_gain = jnp.sum(d_gated * state_hat * gate_act, 0)
    d_gate_raw = (
        d_gated * state_hat * gain_out * (gate_sig * (1.0 + gate_raw * (1.0 - gate_sig)))
    ).astype(BF16)
    d_state_hat = d_gated * gain_out * gate_act
    gate_out_term = t_dot(normed, d_gate_raw).astype(BF16)
    state_dot = sum_group(jnp.sum(d_state_hat * state_hat, 1), (gate_out_term,))[:, None] / full
    d_state = scale_state * (d_state_hat - state_hat * state_dot)
    back_decay, back_run, back_decay_all, back_run_all = linear_scan(
        forget.reshape(shape3), (forget * d_state).reshape(shape3), True
    )
    d_resid_all = jnp.concatenate(d_resids, 0)
    gated_all = jnp.concatenate([rows_of(gated, q ^ k, chunk) for k in range(group)], 0)
    out_term = t_dot(gated_all, d_resid_all).astype(BF16)
    later_in = carry(back_decay_all, back_run_all, True, (out_term,))
    adjoint = d_state + (back_run + back_decay * later_in).reshape(rows, width)
    d_in = (adjoint * (1.0 - forget) * (in_sig * (1.0 + in_raw * (1.0 - in_sig)))).astype(BF16)
    d_forget = (
        (adjoint * prev - adjoint * in_act) * (1.0 - lower) * forget_sig * (1.0 - forget_sig)
    ).astype(BF16)
    down_ready = combine(after(down_sum, d_gated), back_run_all, later_in)
    d_in_here = after(d_in, down_ready)
    d_terms = {
        k: dot_t(d_in_here, rows_of(w_in, v ^ k, width))
        + dot_t(d_forget, rows_of(w_fg, v ^ k, width))
        + dot_t(d_gate_raw, rows_of(w_go, v ^ k, width))
        for k in remote_first
    }
    both_term = t_dot(normed, after(jnp.concatenate((d_in, d_forget), 1), d_terms[1])).astype(BF16)
    in_term, forget_term = (both_term[:, :width], both_term[:, width:])
    pair_ready = combine(after(pair_sum, d_in), d_terms[1], d_terms[0])
    mixed, _ = scatter_group(outs, (state_dot,), (later_in,))
    mixed = (resid + mixed).astype(BF16)
    arrived = {0: cols_of(mixed, v, width)}
    for k in range(1, group):
        pairs = [
            (place(core, at), place(core ^ (k // half), at ^ (k % half)))
            for core in range(2)
            for at in range(n_mp)
        ]
        arrived[k] = after(
            lax.ppermute(cols_of(mixed, v ^ k, width), ("dp", "mp"), pairs), d_terms[1]
        )
    mixed = join(
        [arrived[k] for k in range(group)], lambda k: q ^ k, chunk, (rows, width), 0, BF16
    )
    vectors = jnp.zeros((2, full), F32)
    vectors = lax.dynamic_update_slice(vectors, grad_out_gain[None], (0, q * width))
    vectors = lax.dynamic_update_slice(vectors, grad_norm_mid[None], (1, 0))
    vectors = lax.psum(after(vectors, later_in), ("seq", "dp", "mp"))
    vectors = lax.dynamic_slice_in_dim(vectors, m * width, width, 1)
    mixed_here = mixed
    mixed_there = lax.ppermute(mixed, ("dp", "mp"), crossing)

    d_normed, d_normed_sent = scatter_group(d_terms, (), (both_term, d_terms[0], mixed_here, pair_ready))
    gain_here = small_of(v, 0)
    x_hat = x_own.astype(F32) * scale_in
    grad_norm_in = jnp.sum(d_normed * x_hat, 0)
    d_x_hat = d_normed * gain_here
    in_dot = sum_group(jnp.sum(d_x_hat * x_hat, 1))[:, None] / full
    d_resid_here = join(
        [cols_of(value, v, width) for value in d_resids],
        lambda k: q ^ k,
        chunk,
        (rows, width),
        0,
        BF16,
    )
    d_tokens = d_resid_here.astype(F32) + scale_in * (d_x_hat - x_hat * in_dot)
    d_tokens_there = lax.ppermute(d_tokens.astype(BF16), ("dp", "mp"), crossing)

    mixed = jnp.where(c == part, mixed_here, after(mixed_there, d_normed))

    def gates_of(*gates):
        return (gates[0],) * (seq_bits - 1) + (gates[1],)

    out_sum = sync(after(out_term, later_in), straight, gates_of(d_terms[0], forget_term))
    go_sum = sync(after(gate_out_term, later_in), crossed, gates_of(d_terms[0], forget_term))
    in_sum = sync(in_term, straight, gates_of(d_terms[0], d_normed))
    forget_sum = sync(forget_term, crossed, gates_of(d_terms[0], d_normed))
    grad_down = spread(down_ready)
    grad_pair = spread(pair_ready)
    mix_sum = jnp.concatenate((in_sum, forget_sum, go_sum), 1)
    mix_ready = combine(after(mix_sum, pair_ready), in_dot, in_dot)
    out_ready = combine(after(out_sum, pair_ready), in_dot, in_dot)
    grad_mix = spread(mix_ready)
    grad_out = spread(out_ready)

    for bit in bits_of(n_seq):
        there = lax.ppermute(grad_norm_in, "seq", [(i, i ^ bit) for i in range(n_seq)])
        grad_norm_in = grad_norm_in + there
    other_half = lax.ppermute(grad_norm_in, "mp", [(i, i ^ half) for i in range(n_mp)])
    grad_norm_in = grad_norm_in + other_half
    other_core = lax.ppermute(grad_norm_in, "dp", [(0, 1), (1, 0)])
    grad_norm_in = jnp.where(c == part, grad_norm_in, other_core)

    d_tokens = jnp.where(c == part, d_tokens, d_tokens_there.astype(F32))

    return (
        mixed.reshape(seqs, length, width),
        d_tokens.reshape(seqs, length, width),
        grad_norm_in,
        grad_mix[:, :width].astype(F32),
        grad_mix[:, width : 2 * width].astype(F32),
        grad_mix[:, 2 * width :].astype(F32),
        vectors[0],
        grad_out.astype(F32),
        vectors[1],
        grad_pair[:, :ff].astype(F32),
        grad_pair[:, ff:].astype(F32),
        grad_down.astype(F32),
    )


def solution(mesh):
    acts = P("dp", "seq", "mp")
    cols, rows, vec = (P(None, "mp"), P("mp", None), P("mp"))
    in_specs = (acts, acts, P("dp"), P(), vec, vec, cols, cols, cols, vec, rows, vec, cols, cols, rows)
    out_specs = (acts, acts, vec, cols, cols, cols, vec, rows, vec, cols, cols, rows)
    return jax.shard_map(
        per_device, mesh=mesh, in_specs=in_specs, out_specs=out_specs, check_vma=False
    )
```

time: 3220 us -> 1270 us (0.39)
  waiting for transfers between devices: 1790 us -> 473 us
  local copies, waits for them, and re-layouts: 679 us -> 51.6 us
  blocking collectives: 216 us -> 104 us
  starting transfers between devices: 0.37 us -> 98 us
  Pallas kernels: 0 us -> 33.7 us
    reduce_scatter x3 -> x2, waiting for transfers between devices: 662 us -> 0.01 us  [scatter_seq(): return lax.psum_scatter(value, 'seq', scatter_dimension=0, tiled=True)]
    psum x1 -> x0, waiting for transfers between devices: 569 us -> none  [per_device(): lax.psum((grad_norm_in, grad_w_mix[:, :own_width], grad_w_mix[:, own_widt...]
    all_gather x5 -> x8, waiting for transfers between devices: 563 us -> 0.04 us  [the longest x4 0.04 us: fetch_end(): there = lax.all_gather(piece, ('seq', 'dp'), axis=0, tiled=True)]
    ppermute x0 -> x70, waiting for transfers between devices: none -> 472 us  [the longest x11 202 us: hop(): return lax.ppermute(value, 'mp', [(i, i ^ bit) for i in range(n_mp)])]
    slice x125 -> x7, local copies, waits for them, and re-layouts: 432 us -> 1.18 us  [the longest x1 0.65 us: per_device(): vectors[1]]
    all_to_all x1 -> x0, blocking collectives: 104 us -> none  [per_device(): lax.all_to_all(w_out, 'mp', split_axis=1, concat_axis=0, tiled=True)]
    add x69 -> x11, other arithmetic: 113 us -> 9.77 us  [the longest x1 5.38 us: scatter_group(): live[k ^ bit] = live[k ^ bit] + received.astype(F32)]
    ppermute x0 -> x70, starting transfers between devices: none -> 97.4 us  [the longest x19 27.8 us: hop(): return lax.ppermute(value, 'dp', [(0, 1), (1, 0)])]
  transfers between devices with their start and end apart: 9 -> 80, of which waited for: 9 -> 25; matrix products, arithmetic and copies ran while one was open for 9% -> 36% of each run, Pallas kernels for 0% -> 3%
where the time goes in v1:
time: 1270 us; the launch traced here: 1260 us
  waiting for transfers between devices  473 us (37%)
  matrix products  303 us (24%)
  other arithmetic  184 us (14%)
  blocking collectives  104 us (8%)
  starting transfers between devices  98 us (8%)
  local copies, waits for them, and re-layouts  51.6 us (4%)
  Pallas kernels  33.7 us (3%)
  between operations  16.6 us (1%)
    ppermute x11, waiting for transfers between devices, hop(): return lax.ppermute(value, 'mp', [(i, i ^ bit) for i in range(n_mp)])  202 us
    ppermute x4, waiting for transfers between devices, fetch_start(): lax.ppermute(jnp.concatenate(pieces, 1), 'mp', [(i, i ^ half) for i in ra...  150 us
    dot_general x28, matrix products, dot_t(): lax.dot_general(left, right, (((1,), (1,)), ((), ())), preferred_element_...  121 us
    psum x1, blocking collectives, per_device(): vectors = lax.psum(after(vectors, later_in), ('seq', 'dp', 'mp'))  104 us
    dot_general x19, matrix products, dot(): return jnp.dot(left, right, preferred_element_type=F32)  100 us
    dot_general x5, matrix products, t_dot(): lax.dot_general(left, right, (((0,), (0,)), ((), ())), preferred_element_...  81.7 us
    ppermute x4, waiting for transfers between devices, combine(): lax.ppermute(value, ('dp', 'mp'), [(place(1, i), place(0, i ^ half)) for...  55.9 us
    ppermute x8, waiting for transfers between devices, sync(): away = lax.ppermute(away, 'seq', [(i, i ^ 1 << bit) for i in range(n_seq)])  39.6 us
  transfers between devices with their start and end apart: 80, of which 25 were waited for; matrix products, arithmetic and copies ran while one was open for 36% of the time, Pallas kernels for 3%

profile of v1, /device:TPU:0, one launch (start us, length us, event | category | flops | bytes accessed | tf_op | source)
XLA Modules:
  0.0 1262.9 jit_solution(11276379476445330297)
XLA Ops:
  18.9 74.7 %collective-permute-done = bf16[256,1536]{1,0:T(8,128)(2,1)S(1)} collective-permute-done((bf16[256,1536]{1,0:T(8,128)(2,1)}, bf16[256,1536]{1,0:T(8,128)(2,1)S(1)}, u32[]{:S(2)}, u32[]{:S(2)}) %collective-permute-start) | collective-permute-done | bytes 786464 | tf_op jit(solution)/shard_map/ppermute | solution.py:183
  101.3 75.5 %collective-permute-done.2 = bf16[64,2048]{1,0:T(8,128)(2,1)} collective-permute-done((bf16[64,2048]{1,0:T(8,128)(2,1)S(1)}, bf16[64,2048]{1,0:T(8,128)(2,1)}, u32[]{:S(2)}, u32[]{:S(2)}) %collective-permute-start.2) | collective-permute-done | bytes 262176 | tf_op jit(solution)/shard_map/ppermute | solution.py:183
  216.1 8.1 subtract_multiply_fusion.1
  224.2 16.0 %scan_fwd.1 = (f32[4,512,512]{2,1,0:T(8,128)}, f32[4,512,512]{2,1,0:T(8,128)}, f32[4,1,512]{2,1,0:T(1,128)}, f32[4,1,512]{2,1,0:T(1,128)}) custom-call(f32[4,512,512]{2,1,0:T(8,128)} %bitcast.203, f32[4,512,512]{2,1,0:T(8,128)} %bitcast.228), custom_call_target="tpu_custom_call" | custom-call | tf_op jit(solution)/shard_map/scan_fwd/pallas_call | solution.py:52
  250.1 10.6 fusion.144
  306.4 13.2 %slice_select_fusion = (bf16[2048,1408]{1,0:T(8,128)(2,1)}, bf16[2048,1408]{1,0:T(8,128)(2,1)}) fusion(bf16[2048,1408]{1,0:T(8,128)(2,1)} %param.28, bf16[2048,2816]{1,0:T(8,128)(2,1)} %all-gather.13.cloned.1.call-done, pred[]{:T(512)S(6)} %eq.15, bf16[2048,1408]{1,0:T(8,128)(2,1)} %param.27), kind=kLoop, calls=%fused_computation.37 | loop fusion | flops 5767168 | bytes 34603008 | tf_op jit(solution)/shard_map/jit(_where)/select_n | solution.py:190
  319.6 66.8 %collective-permute-done.17 = bf16[512,2048]{1,0:T(8,128)(2,1)S(1)} collective-permute-done((bf16[512,2048]{1,0:T(8,128)(2,1)}, bf16[512,2048]{1,0:T(8,128)(2,1)S(1)}, u32[]{:S(2)}, u32[]{:S(2)}) %collective-permute-start.17) | collective-permute-done | bytes 2097184 | tf_op jit(solution)/shard_map/ppermute | solution.py:123
  415.1 34.9 %collective-permute-done.24 = bf16[512,2048]{1,0:T(8,128)(2,1)} collective-permute-done((bf16[512,2048]{1,0:T(8,128)(2,1)S(1)}, bf16[512,2048]{1,0:T(8,128)(2,1)}, u32[]{:S(2)}, u32[]{:S(2)}) %collective-permute-start.24) | collective-permute-done | bytes 2097184 | tf_op jit(solution)/shard_map/ppermute | solution.py:123
  466.7 26.5 %collective-permute-done.20 = bf16[2048,512]{1,0:T(8,128)(2,1)S(1)} collective-permute-done((bf16[2048,512]{1,0:T(8,128)(2,1)S(1)}, bf16[2048,512]{1,0:T(8,128)(2,1)S(1)}, u32[]{:S(2)}, u32[]{:S(2)}) %collective-permute-start.20) | collective-permute-done | bytes 2097184 | tf_op jit(solution)/shard_map/ppermute | solution.py:123
  524.7 7.4 multiply_convert_fusion.7
  542.1 7.3 multiply_convert_fusion.13
  564.8 7.3 multiply_convert_fusion.9
  595.5 18.1 %fusion.35 = bf16[1408,2048]{1,0:T(8,128)(2,1)} fusion(bf16[512,2048]{1,0:T(8,128)(2,1)} %get-tuple-element.201, bf16[512,2048]{1,0:T(8,128)(2,1)} %copy-done.67, bf16[512,2048]{1,0:T(8,128)(2,1)} %get-tuple-element.200, bf16[512,2048]{1,0:T(8,128)(2,1)} %get-tuple-element.121, bf16[512,1408]{1,0:T(8,128)(2,1)} %get-tuple-element.136, ...), kind=kOutput, calls=%fused_computation.34 | convolution fusion | flops 11870666752 | bytes 19922944 | tf_op jit(solution)/shard_map/dot_general | solution.py:71
  620.9 22.7 %collective-permute-done.28 = bf16[512,2048]{1,0:T(8,128)(2,1)} collective-permute-done((bf16[512,2048]{1,0:T(8,128)(2,1)}, bf16[512,2048]{1,0:T(8,128)(2,1)}, u32[]{:S(2)}, u32[]{:S(2)}) %collective-permute-start.28) | collective-permute-done | bytes 2097184 | tf_op jit(solution)/shard_map/ppermute | solution.py:123
  652.3 39.2 %fusion.16 = bf16[2048,2816]{1,0:T(8,128)(2,1)} fusion(bf16[2048,2048]{1,0:T(8,128)(2,1)} %pad_maximum_fusion, bf16[512,1408]{1,0:T(8,128)(2,1)} %get-tuple-element.214, bf16[512,1408]{1,0:T(8,128)(2,1)} %copy-done.111, bf16[512,1408]{1,0:T(8,128)(2,1)} %get-tuple-element.208, bf16[512,1408]{1,0:T(8,128)(2,1)} %copy-done.113, ...), kind=kOutput, calls=%fused_computation.16 | convolution fusion | flops 23720361984 | bytes 31457280 | tf_op jit(solution)/shard_map/dot_general | solution.py:71
  691.7 7.9 collective-permute-done.29
  736.9 9.0 fusion.74
  750.8 17.7 %scan_back.1 = (f32[4,512,512]{2,1,0:T(8,128)}, f32[4,512,512]{2,1,0:T(8,128)}, f32[4,1,512]{2,1,0:T(1,128)}, f32[4,1,512]{2,1,0:T(1,128)}) custom-call(f32[4,512,512]{2,1,0:T(8,128)} %bitcast.204, f32[4,512,512]{2,1,0:T(8,128)} %bitcast.205), custom_call_target="tpu_custom_call" | custom-call | tf_op jit(solution)/shard_map/scan_back/pallas_call | solution.py:52
  823.5 33.5 %collective-permute-done.36 = bf16[512,2048]{1,0:T(8,128)(2,1)} collective-permute-done((bf16[512,2048]{1,0:T(8,128)(2,1)}, bf16[512,2048]{1,0:T(8,128)(2,1)}, u32[]{:S(2)}, u32[]{:S(2)}) %collective-permute-start.36) | collective-permute-done | bytes 2097184 | tf_op jit(solution)/shard_map/ppermute | solution.py:123
  881.6 10.5 convolution_convert_fusion
  892.3 7.6 add_add_fusion
  919.0 12.1 collective-permute-done.40
  931.1 21.5 %collective-permute-start.46 = (bf16[2048,512]{1,0:T(8,128)(2,1)S(1)}, bf16[2048,512]{1,0:T(8,128)(2,1)S(1)}, u32[]{:S(2)}, u32[]{:S(2)}) collective-permute-start(bf16[2048,512]{1,0:T(8,128)(2,1)S(1)} %copy-done.58), channel_id=1, source_target_pairs={{0,4},{4,0},{1,5},{5,1},{2,6},{6,2},{3,7},{7,3},{8,12},{12,8},{9,1... | collective-permute-start | bytes 6291464 | tf_op jit(solution)/shard_map/ppermute | solution.py:122
  957.1 17.0 %collective-permute-done.49 = bf16[512,2816]{1,0:T(8,128)(2,1)S(1)} collective-permute-done((bf16[512,2816]{1,0:T(8,128)(2,1)}, bf16[512,2816]{1,0:T(8,128)(2,1)S(1)}, u32[]{:S(2)}, u32[]{:S(2)}) %collective-permute-start.49) | collective-permute-done | bytes 2883616 | tf_op jit(solution)/shard_map/ppermute | solution.py:212
  979.9 9.5 collective-permute-done.63
  994.4 21.0 %collective-permute-done.60 = bf16[2,512,512]{2,1,0:T(8,128)(2,1)S(1)} collective-permute-done((bf16[2,512,512]{2,1,0:T(8,128)(2,1)S(1)}, bf16[2,512,512]{2,1,0:T(8,128)(2,1)S(1)}, u32[]{:S(2)}, u32[]{:S(2)}) %collective-permute-start.60) | collective-permute-done | bytes 1048608 | tf_op jit(solution)/shard_map/ppermute | solution.py:206
  1039.5 9.0 collective-permute-done.61
  1052.1 38.2 %collective-permute-done.64 = bf16[512,1536]{1,0:T(8,128)(2,1)S(1)} collective-permute-done((bf16[512,1536]{1,0:T(8,128)(2,1)S(1)}, bf16[512,1536]{1,0:T(8,128)(2,1)S(1)}, u32[]{:S(2)}, u32[]{:S(2)}) %collective-permute-start.64) | collective-permute-done | bytes 1572896 | tf_op jit(solution)/shard_map/ppermute | solution.py:212
  1110.8 103.6 %psum.7 = f32[2,2048]{1,0:T(2,128)S(1)} all-reduce(f32[2,2048]{1,0:T(2,128)S(1)} %dynamic_update_slice.103), channel_id=1, replica_groups=mesh['seq'=4,'dp'=2,'mp'=4] {'seq','dp','mp'}, use_global_device_ids=true, to_apply=%region_15.16 | all-reduce | flops 4096 | bytes 32768 | tf_op jit(solution)/shard_map/psum | solution.py:430
  1215.9 8.8 convert_element_type.489
  1236.6 8.1 slice_convert_fusion.2
  1244.7 11.1 slice_convert_fusion
  (624 shorter events, 471.6 us)
Async XLA Ops:
  7.2 185.2 %all-gather.9.cloned.1.call-start = ((), (), s32[]{:S(2)}) async-start(), calls=%async_computation.2 | async-start | bytes 7077888 | tf_op jit(solution)/shard_map/all_gather | solution.py:186
  13.1 80.5 %collective-permute-start = (bf16[256,1536]{1,0:T(8,128)(2,1)}, bf16[256,1536]{1,0:T(8,128)(2,1)S(1)}, u32[]{:S(2)}, u32[]{:S(2)}) collective-permute-start(bf16[256,1536]{1,0:T(8,128)(2,1)} %pad_maximum_fusion.4), channel_id=1, source_target_pairs={{0,2},{1,3},{2,0},{3,1},{4,6},{5,7},{6,4},{7,5},{8,10},{9,11},{10,... | collective-permute-start | bytes 2359304 | tf_op jit(solution)/shard_map/ppermute | solution.py:183
  94.5 178.4 %all-gather.11.cloned.1.call-start = ((), (), s32[]{:S(2)}) async-start(), calls=%async_computation.3 | async-start | bytes 2359296 | tf_op jit(solution)/shard_map/all_gather | solution.py:186
  94.5 83.1 %collective-permute-start.4 = (bf16[2048,512]{1,0:T(8,128)(2,1)S(1)}, bf16[2048,512]{1,0:T(8,128)(2,1)}, u32[]{:S(2)}, u32[]{:S(2)}) collective-permute-start(bf16[2048,512]{1,0:T(8,128)(2,1)S(1)} %broadcast_select_fusion.4), channel_id=1, source_target_pairs={{0,1},{1,0},{2,3},{3,2},{4,5},{5,4},{6,7},{7,6},{8,9},{9,8},{10,11... | collective-permute-start | bytes 6291464 | tf_op jit(solution)/shard_map/ppermute | solution.py:123
  97.3 79.5 %collective-permute-start.3 = (bf16[256,2816]{1,0:T(8,128)(2,1)}, bf16[256,2816]{1,0:T(8,128)(2,1)S(1)}, u32[]{:S(2)}, u32[]{:S(2)}) collective-permute-start(bf16[256,2816]{1,0:T(8,128)(2,1)} %pad_maximum_fusion.3), channel_id=1, source_target_pairs={{0,2},{1,3},{2,0},{3,1},{4,6},{5,7},{6,4},{7,5},{8,10},{9,11},{10,... | collective-permute-start | bytes 4325384 | tf_op jit(solution)/shard_map/ppermute | solution.py:183
  98.3 78.5 %collective-permute-start.2 = (bf16[64,2048]{1,0:T(8,128)(2,1)S(1)}, bf16[64,2048]{1,0:T(8,128)(2,1)}, u32[]{:S(2)}, u32[]{:S(2)}) collective-permute-start(bf16[64,2048]{1,0:T(8,128)(2,1)S(1)} %constant_dynamic-slice_fusion.25), channel_id=1, source_target_pairs={{0,2},{1,3},{2,0},{3,1},{4,6},{5,7},{6,4},{7,5},{8,10},{9,11},{10,... | collective-permute-start | bytes 786440 | tf_op jit(solution)/shard_map/ppermute | solution.py:183
  177.7 128.7 %all-gather.13.cloned.1.call-start = ((), (), s32[]{:S(2)}) async-start(), calls=%async_computation.4 | async-start | bytes 12976128 | tf_op jit(solution)/shard_map/all_gather | solution.py:186
  178.4 335.2 %all-gather.15.cloned.1.call-start = ((), (), s32[]{:S(2)}) async-start(), calls=%async_computation.5 | async-start | bytes 6488064 | tf_op jit(solution)/shard_map/all_gather | solution.py:186
  300.5 85.9 %collective-permute-start.17 = (bf16[512,2048]{1,0:T(8,128)(2,1)}, bf16[512,2048]{1,0:T(8,128)(2,1)S(1)}, u32[]{:S(2)}, u32[]{:S(2)}) collective-permute-start(bf16[512,2048]{1,0:T(8,128)(2,1)} %add_convert_fusion.9), channel_id=1, source_target_pairs={{0,1},{1,0},{2,3},{3,2},{4,5},{5,4},{6,7},{7,6},{8,9},{9,8},{10,11... | collective-permute-start | bytes 6291464 | tf_op jit(solution)/shard_map/ppermute | solution.py:123
  303.0 90.1 %collective-permute-start.15 = (bf16[176,2048]{1,0:T(8,128)(2,1)S(1)}, bf16[176,2048]{1,0:T(8,128)(2,1)S(1)}, u32[]{:S(2)}, u32[]{:S(2)}) collective-permute-start(bf16[176,2048]{1,0:T(8,128)(2,1)S(1)} %constant_dynamic-slice_fusion.14), channel_id=1, source_target_pairs={{0,2},{1,3},{2,0},{3,1},{4,6},{5,7},{6,4},{7,5},{8,10},{9,11},{10,... | collective-permute-start | bytes 2162696 | tf_op jit(solution)/shard_map/ppermute | solution.py:183
  304.4 96.9 %collective-permute-start.18 = (bf16[2048,512]{1,0:T(8,128)(2,1)}, bf16[2048,512]{1,0:T(8,128)(2,1)}, u32[]{:S(2)}, u32[]{:S(2)}) collective-permute-start(bf16[2048,512]{1,0:T(8,128)(2,1)} %bitcast.19), channel_id=1, source_target_pairs={{2,4},{3,5},{4,2},{5,3},{10,12},{11,13},{12,10},{13,11},{18,20},{1... | collective-permute-start | bytes 6291464 | tf_op jit(solution)/shard_map/ppermute | solution.py:161
  394.0 414.0 %reduce-scatter.3.cloned.1.call-start = ((), (), s32[]{:S(2)}) async-start(), calls=%async_computation.6 | async-start | bytes 7208960 | tf_op jit(solution)/shard_map/reduce_scatter | solution.py:368
  412.8 80.4 %collective-permute-start.20 = (bf16[2048,512]{1,0:T(8,128)(2,1)S(1)}, bf16[2048,512]{1,0:T(8,128)(2,1)S(1)}, u32[]{:S(2)}, u32[]{:S(2)}) collective-permute-start(bf16[2048,512]{1,0:T(8,128)(2,1)S(1)} %broadcast_select_fusion.3), channel_id=1, source_target_pairs={{0,1},{1,0},{2,3},{3,2},{4,5},{5,4},{6,7},{7,6},{8,9},{9,8},{10,11... | collective-permute-start | bytes 6291464 | tf_op jit(solution)/shard_map/ppermute | solution.py:123
  414.2 79.4 %collective-permute-start.21 = (bf16[2048,512]{1,0:T(8,128)(2,1)S(1)}, bf16[2048,512]{1,0:T(8,128)(2,1)S(1)}, u32[]{:S(2)}, u32[]{:S(2)}) collective-permute-start(bf16[2048,512]{1,0:T(8,128)(2,1)S(1)} %broadcast_select_fusion.3), channel_id=1, source_target_pairs={{0,4},{4,0},{1,5},{5,1},{2,6},{6,2},{3,7},{7,3},{8,12},{12,8},{9,1... | collective-permute-start | bytes 6291464 | tf_op jit(solution)/shard_map/ppermute | solution.py:122
  613.7 293.0 %reduce-scatter.5.cloned.1.call-start = ((), (), s32[]{:S(2)}) async-start(), calls=%async_computation.7 | async-start | bytes 14417920 | tf_op jit(solution)/shard_map/reduce_scatter | solution.py:368
  691.6 524.3 %all-gather.23.cloned.1.call-start = ((), (), s32[]{:S(2)}) async-start(), calls=%async_computation.11 | async-start | bytes 6488064 | tf_op jit(solution)/shard_map/all_gather | solution.py:221
  721.2 102.3 %collective-permute-start.32 = (bf16[512,2048]{1,0:T(8,128)(2,1)}, bf16[512,2048]{1,0:T(8,128)(2,1)}, u32[]{:S(2)}, u32[]{:S(2)}) collective-permute-start(bf16[512,2048]{1,0:T(8,128)(2,1)} %convolution_convert_fusion.5), channel_id=1, source_target_pairs={{0,4},{4,0},{1,5},{5,1},{2,6},{6,2},{3,7},{7,3},{8,12},{12,8},{9,1... | collective-permute-start | bytes 6291464 | tf_op jit(solution)/shard_map/ppermute | solution.py:122
  736.3 54.0 %collective-permute-start.35 = (bf16[512,2048]{1,0:T(8,128)(2,1)}, bf16[512,2048]{1,0:T(8,128)(2,1)}, u32[]{:S(2)}, u32[]{:S(2)}) collective-permute-start(bf16[512,2048]{1,0:T(8,128)(2,1)} %convolution_convert_fusion.4), channel_id=1, source_target_pairs={{0,4},{4,0},{1,5},{5,1},{2,6},{6,2},{3,7},{7,3},{8,12},{12,8},{9,1... | collective-permute-start | bytes 6291464 | tf_op jit(solution)/shard_map/ppermute | solution.py:122
  781.0 130.0 %collective-permute-start.66 = (bf16[2,128,2048]{2,1,0:T(8,128)(2,1)}, bf16[2,128,2048]{2,1,0:T(8,128)(2,1)}, u32[]{:S(2)}, u32[]{:S(2)}) collective-permute-start(bf16[2,128,2048]{2,1,0:T(8,128)(2,1)} %dynamic-slice_bitcast_fusion), channel_id=1, source_target_pairs={{0,8},{8,0},{16,24},{24,16},{1,9},{9,1},{17,25},{25,17},{2,10},{10... | collective-permute-start | bytes 3145736 | tf_op jit(solution)/shard_map/ppermute | solution.py:206
  784.7 168.2 %collective-permute-start.62 = (bf16[2,512,512]{2,1,0:T(8,128)(2,1)}, bf16[2,512,512]{2,1,0:T(8,128)(2,1)S(1)}, u32[]{:S(2)}, u32[]{:S(2)}) collective-permute-start(bf16[2,512,512]{2,1,0:T(8,128)(2,1)} %dynamic-slice_bitcast_fusion.1), channel_id=1, source_target_pairs={{0,16},{8,24},{16,0},{24,8},{1,17},{9,25},{17,1},{25,9},{2,18},{10... | collective-permute-start | bytes 3145736 | tf_op jit(solution)/shard_map/ppermute | solution.py:206
  794.8 62.2 %collective-permute-start.36 = (bf16[512,2048]{1,0:T(8,128)(2,1)}, bf16[512,2048]{1,0:T(8,128)(2,1)}, u32[]{:S(2)}, u32[]{:S(2)}) collective-permute-start(bf16[512,2048]{1,0:T(8,128)(2,1)} %add_convert_fusion.5), channel_id=1, source_target_pairs={{0,1},{1,0},{2,3},{3,2},{4,5},{5,4},{6,7},{7,6},{8,9},{9,8},{10,11... | collective-permute-start | bytes 6291464 | tf_op jit(solution)/shard_map/ppermute | solution.py:123
  808.0 49.0 %collective-permute-start.41 = (bf16[352,2048]{1,0:T(8,128)(2,1)}, bf16[352,2048]{1,0:T(8,128)(2,1)S(1)}, u32[]{:S(2)}, u32[]{:S(2)}) collective-permute-start(bf16[352,2048]{1,0:T(8,128)(2,1)} %reduce-scatter.3.cloned.1.call-done), channel_id=1, source_target_pairs={{4,2},{5,3},{6,0},{7,1},{12,10},{13,11},{14,8},{15,9},{20,18},{21,... | collective-permute-start | bytes 4325384 | tf_op jit(solution)/shard_map/ppermute | solution.py:212
  866.0 52.6 %collective-permute-start.43 = (bf16[512,512]{1,0:T(8,128)(2,1)}, bf16[512,512]{1,0:T(8,128)(2,1)}, u32[]{:S(2)}, u32[]{:S(2)}) collective-permute-start(bf16[512,512]{1,0:T(8,128)(2,1)} %get-tuple-element.221), channel_id=1, source_target_pairs={{0,4},{1,5},{2,6},{3,7},{4,0},{5,1},{6,2},{7,3},{8,12},{9,13},{10,... | collective-permute-start | bytes 1572872 | tf_op jit(solution)/shard_map/ppermute | solution.py:422
  892.1 340.3 %all-gather.19.cloned.1.call-start = ((), (), s32[]{:S(2)}) async-start(), calls=%async_computation.9 | async-start | bytes 2359296 | tf_op jit(solution)/shard_map/all_gather | solution.py:221
  906.6 67.5 %collective-permute-start.49 = (bf16[512,2816]{1,0:T(8,128)(2,1)}, bf16[512,2816]{1,0:T(8,128)(2,1)S(1)}, u32[]{:S(2)}, u32[]{:S(2)}) collective-permute-start(bf16[512,2816]{1,0:T(8,128)(2,1)} %reduce-scatter.5.cloned.1.call-done), channel_id=1, source_target_pairs={{4,2},{5,3},{6,0},{7,1},{12,10},{13,11},{14,8},{15,9},{20,18},{21,... | collective-permute-start | bytes 8650760 | tf_op jit(solution)/shard_map/ppermute | solution.py:212
  918.6 59.9 %collective-permute-start.67 = (bf16[128,2048]{1,0:T(8,128)(2,1)}, bf16[128,2048]{1,0:T(8,128)(2,1)S(1)}, u32[]{:S(2)}, u32[]{:S(2)}) collective-permute-start(bf16[128,2048]{1,0:T(8,128)(2,1)} %dynamic-slice_bitcast_fusion.4), channel_id=1, source_target_pairs={{0,16},{8,24},{16,0},{24,8},{1,17},{9,25},{17,1},{25,9},{2,18},{10... | collective-permute-start | bytes 1572872 | tf_op jit(solution)/shard_map/ppermute | solution.py:206
  931.1 84.4 %collective-permute-start.46 = (bf16[2048,512]{1,0:T(8,128)(2,1)S(1)}, bf16[2048,512]{1,0:T(8,128)(2,1)S(1)}, u32[]{:S(2)}, u32[]{:S(2)}) collective-permute-start(bf16[2048,512]{1,0:T(8,128)(2,1)S(1)} %copy-done.58), channel_id=1, source_target_pairs={{0,4},{4,0},{1,5},{5,1},{2,6},{6,2},{3,7},{7,3},{8,12},{12,8},{9,1... | collective-permute-start | bytes 6291464 | tf_op jit(solution)/shard_map/ppermute | solution.py:122
  1049.4 187.1 %all-gather.17.cloned.1.call-start = ((), (), s32[]{:S(2)}) async-start(), calls=%async_computation.8 | async-start | bytes 7077888 | tf_op jit(solution)/shard_map/all_gather | solution.py:221
  1094.9 149.8 %all-gather.21.cloned.1.call-start = ((), (), s32[]{:S(2)}) async-start(), calls=%async_computation.10 | async-start | bytes 12976128 | tf_op jit(solution)/shard_map/all_gather | solution.py:221
  1099.1 125.6 %collective-permute-start.45 = (bf16[2048,512]{1,0:T(8,128)(2,1)}, bf16[2048,512]{1,0:T(8,128)(2,1)}, u32[]{:S(2)}, u32[]{:S(2)}) collective-permute-start(bf16[2048,512]{1,0:T(8,128)(2,1)} %copy-done.37), channel_id=1, source_target_pairs={{2,4},{3,5},{4,2},{5,3},{10,12},{11,13},{12,10},{13,11},{18,20},{1... | collective-permute-start | bytes 6291464 | tf_op jit(solution)/shard_map/ppermute | solution.py:433
  1104.6 122.4 %collective-permute-start.53 = (bf16[2048,512]{1,0:T(8,128)(2,1)}, bf16[2048,512]{1,0:T(8,128)(2,1)}, u32[]{:S(2)}, u32[]{:S(2)}) collective-permute-start(bf16[2048,512]{1,0:T(8,128)(2,1)} %fusion.138), channel_id=1, source_target_pairs={{2,4},{3,5},{4,2},{5,3},{10,12},{11,13},{12,10},{13,11},{18,20},{1... | collective-permute-start | bytes 6291464 | tf_op jit(solution)/shard_map/ppermute | solution.py:450
  1110.2 104.2 %collective-permute-start.55 = (f32[512]{0:T(512)S(1)}, f32[512]{0:T(512)S(1)}, u32[]{:S(2)}, u32[]{:S(2)}) collective-permute-start(f32[512]{0:T(512)S(1)} %add.554), channel_id=1, source_target_pairs={{0,16},{8,24},{16,0},{24,8},{1,17},{9,25},{17,1},{25,9},{2,18},{10... | collective-permute-start | bytes 6152 | tf_op jit(solution)/shard_map/ppermute | solution.py:470
  (188 other events, 3123.3 us)
Sparse Core Ops, SparseCore 0:
  94.6 45.8 all-gather.8
  177.8 28.1 all-gather.10
  207.9 67.6 all-gather.12
  394.1 41.3 all-gather.14
  613.8 64.4 reduce-scatter.2
  691.7 127.3 reduce-scatter.4
  892.2 50.6 all-gather.22
  1049.6 27.7 all-gather.18
  1095.1 44.1 all-gather.16
  1141.6 67.7 all-gather.20
